TPU v7x, 256 devices: a whole 4x4x8 slice. The times are simulated.
256 devices in a mesh: tm: 32 (over y, z), row: 8 (over x, core).
Axes of the slice: x: 4, y: 4, z: 8, core: 2. Of those that a mesh axis runs over, the one named last changes fastest.
Arguments:
- precisions: float32 [32, 1024, 1024], P('tm', 'row'), as said below
- couplings: float32 [32, 1024, 1024], P('tm', 'row'), as said below
- right_sides: float32 [32, 1024, 256], P('tm', 'row'), may hold values from -6 to 6
Outputs:
- pivot_blocks: float32 [32, 1024, 1024], P('tm', 'row')
- coupling_blocks: float32 [32, 1024, 1024], P('tm', 'row')
- reduced_sides: float32 [32, 1024, 256], P('tm', 'row')
Inputs may be any that keep to these rules, and one draw needn't show every extreme that they name: precisions and couplings together form a symmetric positive definite block-tridiagonal matrix whose eigenvalues are 1 or more; couplings[0] is zero. `couplings`: see precisions.
All inputs are finite; a program needn't handle non-finite values.
Results may differ from a plain program's by a relative error of at most 0.00023.
Values sent between devices are 32-bit elements; how exact they have to be, the bound alone decides.
No kernel may reach another device: no remote copies, remote signals or barrier semaphores. Data moves between devices by JAX's collectives and lax.ppermute only.
A program may use at most 128 MiB of HBM per device.

v0:
```python
import jax
import jax.numpy as jnp
from jax import lax
from jax.sharding import PartitionSpec as P

LEVELS = 2


def from_behind(block, axis, distance):
    devices = range(lax.axis_size(axis))
    route = [(i - distance, i) for i in devices if i - distance in devices]
    return lax.ppermute(block, axis, route)


def contract(left, right):
    return lax.dot_general(left, right, (((0,), (0,)), ((), ())), precision=lax.Precision.HIGHEST)


def split_cholesky(matrix):
    order = matrix.shape[0]
    if order <= 512:
        return jnp.linalg.cholesky(matrix)
    half = order // 2
    upper_factor = split_cholesky(matrix[:half, :half])
    solved_cols = jax.scipy.linalg.solve_triangular(upper_factor, matrix[:half, half:], lower=True)
    lower_left = solved_cols.T
    remainder = matrix[half:, half:] - contract(solved_cols, solved_cols)
    lower_factor = split_cholesky(remainder)
    top_rows = jnp.concatenate(
        [upper_factor, jnp.zeros((half, order - half), matrix.dtype)], axis=1
    )
    bottom_rows = jnp.concatenate([lower_left, lower_factor], axis=1)
    return jnp.concatenate([top_rows, bottom_rows], axis=0)


def local(precisions, couplings, right_sides):
    diagonal_pivot_rows = precisions[0]
    offdiag_coupling_rows = couplings[0]
    rhs_side_rows = right_sides[0]
    row_count = diagonal_pivot_rows.shape[0]
    block_position = lax.axis_index("tm")
    row_start = lax.axis_index("row") * row_count
    offdiag_coupling_rows = jnp.where(
        block_position == 0, jnp.zeros_like(offdiag_coupling_rows), offdiag_coupling_rows
    )
    for level_step in range(LEVELS):
        level_stride = 1 << level_step
        whole_pivot, whole_coupling, whole_side = (
            lax.all_gather(diagonal_pivot_rows, "row", axis=0, tiled=True),
            lax.all_gather(offdiag_coupling_rows, "row", axis=0, tiled=True),
            lax.all_gather(rhs_side_rows, "row", axis=0, tiled=True),
        )
        next_coupling = from_behind(whole_coupling, "tm", -level_stride)
        factor = split_cholesky(whole_pivot)
        left_part = jax.scipy.linalg.cho_solve((factor, True), offdiag_coupling_rows.T)
        right_cols = lax.dynamic_slice_in_dim(next_coupling, row_start, row_count, 1)
        right_part = jax.scipy.linalg.cho_solve((factor, True), right_cols)
        left_block = lax.dot_general(
            left_part, whole_coupling, (((0,), (1,)), ((), ())), precision=lax.Precision.HIGHEST
        )
        left_side = contract(left_part, whole_side)
        right_block = contract(right_part, next_coupling)
        right_side = contract(right_part, whole_side)
        new_coupling = -contract(left_part, next_coupling)
        received_following = from_behind((left_block, left_side), "tm", -level_stride)
        received_previous = from_behind((right_block, right_side, new_coupling), "tm", level_stride)
        diagonal_pivot_rows = diagonal_pivot_rows - received_following[0] - received_previous[0]
        rhs_side_rows = rhs_side_rows - received_following[1] - received_previous[1]
        offdiag_coupling_rows = received_previous[2]
    return (diagonal_pivot_rows[None], offdiag_coupling_rows[None], rhs_side_rows[None])


def solution(mesh):
    placed = (P("tm", "row", None), P("tm", "row", None), P("tm", "row", None))
    return jax.shard_map(
        local,
        mesh=mesh,
        in_specs=placed,
        out_specs=(P("tm", "row", None), P("tm", "row", None), P("tm", "row", None)),
        check_vma=False,
    )
```

profile of v0, /device:TPU:8, one launch (start us, length us, event | category | flops | bytes accessed | tf_op | source)
XLA Modules:
  0.0 1219.0 jit_solution(4765637610458641546)
XLA Ops:
  13.9 38.0 %all-gather.16.cloned.1.call-done = f32[1,1024,1024]{1,2,0:T(8,128)} async-done(((f32[1,128,1024]{1,2,0:T(8,128)}), f32[1,1024,1024]{1,2,0:T(8,128)}) %all-gather.16.cloned.1.call-update) | async-done | bytes 4194320 | tf_op jit(solution)/shard_map/all_gather | solution.py:49
  55.0 11.7 cholesky.462
  77.4 11.7 cholesky.481
  99.8 11.7 cholesky.502
  122.6 11.7 cholesky.519
  156.4 39.3 %custom-call.44 = f32[4,128,128]{1,2,0:T(8,128)S(1)} custom-call(f32[4,128,128]{2,1,0:T(8,128)S(1)} %get-tuple-element.46), custom_call_target="InvertDiagBlocksLowerTriangular" | custom-call | tf_op jit(solution)/shard_map/jit(_solve_triangular)/triangular_solve | solution.py:25
  213.0 11.7 cholesky.534
  240.0 13.2 %cholesky.553 = f32[128,128]{1,0:T(8,128)} custom-call(f32[128,128]{1,0:T(8,128)} %cholesky.763), custom_call_target="Cholesky" | custom-call | tf_op jit(solution)/shard_map/jit(cholesky)/cholesky | solution.py:22
  266.8 11.9 cholesky.574
  290.6 11.7 cholesky.591
  308.1 23.2 %while.13 = (s32[]{:T(128)}, f32[1024,1024]{1,0:T(8,128)}, s32[8,2]{0,1:T(2,128)S(1)}, f32[8,128,128]{2,1,0:T(8,128)S(1)}, s32[]{:T(128)}) while((s32[]{:T(128)}, f32[1024,1024]{1,0:T(8,128)}, s32[8,2]{0,1:T(2,128)S(1)}, f32[8,128,128]{2,1,0:T(8,128)S(1)}, s32[]{:T(128)}) %tuple.193), condition=%wide.while_cond.1, body=%wide.while_body.1.sunk | while | flops 2 | bytes 131181 | solution.py:55
  331.3 78.6 %custom-call.48 = f32[8,128,128]{1,2,0:T(8,128)S(1)} custom-call(f32[8,128,128]{2,1,0:T(8,128)S(1)} %get-tuple-element.47), custom_call_target="InvertDiagBlocksLowerTriangular" | custom-call | tf_op jit(solution)/shard_map/jit(_cho_solve)/triangular_solve | solution.py:55
  440.3 66.3 %collective-permute-done.1 = f32[1024,1024]{1,0:T(8,128)S(1)} collective-permute-done((f32[1024,1024]{1,0:T(8,128)}, f32[1024,1024]{1,0:T(8,128)S(1)}, u32[]{:S(2)}, u32[]{:S(2)}) %collective-permute-start.1) | collective-permute-done | bytes 4194336 | tf_op jit(solution)/shard_map/ppermute | solution.py:12
  527.6 14.7 %collective-permute-done.2 = f32[128,1024]{0,1:T(8,128)S(1)} collective-permute-done((f32[128,1024]{0,1:T(8,128)S(1)}, f32[128,1024]{0,1:T(8,128)S(1)}, u32[]{:S(2)}, u32[]{:S(2)}) %collective-permute-start.2) | collective-permute-done | bytes 524320 | tf_op jit(solution)/shard_map/ppermute | solution.py:12
  549.8 14.0 %collective-permute-done.3 = f32[128,1024]{1,0:T(8,128)S(1)} collective-permute-done((f32[128,1024]{1,0:T(8,128)S(1)}, f32[128,1024]{1,0:T(8,128)S(1)}, u32[]{:S(2)}, u32[]{:S(2)}) %collective-permute-start.3) | collective-permute-done | bytes 524320 | tf_op jit(solution)/shard_map/ppermute | solution.py:12
  584.0 11.7 cholesky.606
  606.4 11.7 cholesky.625
  653.2 11.7 cholesky.663
  676.2 39.3 %custom-call.53 = f32[4,128,128]{1,2,0:T(8,128)S(1)} custom-call(f32[4,128,128]{2,1,0:T(8,128)S(1)} %get-tuple-element.49), custom_call_target="InvertDiagBlocksLowerTriangular" | custom-call | tf_op jit(solution)/shard_map/jit(_solve_triangular)/triangular_solve | solution.py:25
  758.8 13.2 %cholesky.697 = f32[128,128]{1,0:T(8,128)} custom-call(f32[128,128]{1,0:T(8,128)} %cholesky.789), custom_call_target="Cholesky" | custom-call | tf_op jit(solution)/shard_map/jit(cholesky)/cholesky | solution.py:22
  785.5 12.1 cholesky.718
  827.1 22.7 %while.15 = (s32[]{:T(128)}, f32[1024,1024]{1,0:T(8,128)}, s32[8,2]{0,1:T(2,128)S(1)}, f32[8,128,128]{2,1,0:T(8,128)S(1)}, s32[]{:T(128)}) while((s32[]{:T(128)}, f32[1024,1024]{1,0:T(8,128)}, s32[8,2]{0,1:T(2,128)S(1)}, f32[8,128,128]{2,1,0:T(8,128)S(1)}, s32[]{:T(128)}) %tuple.216), condition=%wide.while_cond.1.clone.1, body=%wide.while_body.1.clone.1.sunk | while | flops 2 | bytes 131181 | solution.py:55
  849.8 78.8 %custom-call.57 = f32[8,128,128]{1,2,0:T(8,128)S(1)} custom-call(f32[8,128,128]{2,1,0:T(8,128)S(1)} %get-tuple-element.50), custom_call_target="InvertDiagBlocksLowerTriangular" | custom-call | tf_op jit(solution)/shard_map/jit(_cho_solve)/triangular_solve | solution.py:55
  977.8 174.4 %collective-permute-done.5 = f32[1024,1024]{1,0:T(8,128)} collective-permute-done((f32[1024,1024]{1,0:T(8,128)}, f32[1024,1024]{1,0:T(8,128)}, u32[]{:S(2)}, u32[]{:S(2)}) %collective-permute-start.5) | collective-permute-done | bytes 4194336 | tf_op jit(solution)/shard_map/ppermute | solution.py:12
  (520 shorter events, 507.7 us)
Async XLA Ops:
  7.2 44.7 %all-gather.16.cloned.1.call-start = ((), (), s32[]{:S(2)}) async-start(), calls=%async_computation.3 | async-start | bytes 4718592 | tf_op jit(solution)/shard_map/all_gather | solution.py:49
  9.3 400.7 %all-gather.18.cloned.1.call-start = ((), (), s32[]{:S(2)}) async-start(), calls=%async_computation.4 | async-start | bytes 4718592 | tf_op jit(solution)/shard_map/all_gather | solution.py:50
  11.2 553.5 %all-gather.20.cloned.1.call-start = ((), (), s32[]{:S(2)}) async-start(), calls=%async_computation.5 | async-start | bytes 1179648 | tf_op jit(solution)/shard_map/all_gather | solution.py:51
  12.0 568.9 %all-gather.10.cloned.1.call-start = ((), (), s32[]{:S(2)}) async-start(), calls=%async_computation | async-start | bytes 4718592 | tf_op jit(solution)/shard_map/all_gather | solution.py:49
  305.5 110.1 %copy-start.15 = (f32[1024,128]{0,1:T(8,128)S(1)}, f32[1024,128]{0,1:T(8,128)}, u32[]{:S(2)}) copy-start(f32[1024,128]{0,1:T(8,128)} %fusion.497) | copy-start | bytes 1572868
  410.0 96.7 %collective-permute-start.1 = (f32[1024,1024]{1,0:T(8,128)}, f32[1024,1024]{1,0:T(8,128)S(1)}, u32[]{:S(2)}, u32[]{:S(2)}) collective-permute-start(f32[1024,1024]{1,0:T(8,128)} %bitcast.470), channel_id=1, source_target_pairs={{8,0},{16,8},{24,16},{32,24},{40,32},{48,40},{56,48},{64,56},{72,6... | collective-permute-start | bytes 12582920 | tf_op jit(solution)/shard_map/ppermute | solution.py:12
  437.0 90.6 %collective-permute-start = (f32[128,1024]{0,1:T(8,128)S(1)}, f32[128,1024]{0,1:T(8,128)S(1)}, u32[]{:S(2)}, u32[]{:S(2)}) collective-permute-start(f32[128,1024]{0,1:T(8,128)S(1)} %fusion.389), channel_id=1, source_target_pairs={{8,0},{16,8},{24,16},{32,24},{40,32},{48,40},{56,48},{64,56},{72,6... | collective-permute-start | bytes 1572872 | tf_op jit(solution)/shard_map/ppermute | solution.py:12
  525.1 17.3 %collective-permute-start.2 = (f32[128,1024]{0,1:T(8,128)S(1)}, f32[128,1024]{0,1:T(8,128)S(1)}, u32[]{:S(2)}, u32[]{:S(2)}) collective-permute-start(f32[128,1024]{0,1:T(8,128)S(1)} %fusion.395), channel_id=1, source_target_pairs={{0,8},{8,16},{16,24},{24,32},{32,40},{40,48},{48,56},{56,64},{64,7... | collective-permute-start | bytes 1572872 | tf_op jit(solution)/shard_map/ppermute | solution.py:12
  543.2 37.0 %copy-start.17 = (f32[1,128,256]{2,1,0:T(8,128)S(1)}, f32[1,128,256]{2,1,0:T(8,128)}, u32[]{:S(2)}) copy-start(f32[1,128,256]{2,1,0:T(8,128)} %param.10) | copy-start | bytes 393220
  543.2 408.4 %all-gather.12.cloned.1.call-start = ((), (), s32[]{:S(2)}) async-start(), calls=%async_computation.1 | async-start | bytes 4718592 | tf_op jit(solution)/shard_map/all_gather | solution.py:50
  547.9 16.0 %collective-permute-start.3 = (f32[128,1024]{1,0:T(8,128)S(1)}, f32[128,1024]{1,0:T(8,128)S(1)}, u32[]{:S(2)}, u32[]{:S(2)}) collective-permute-start(f32[128,1024]{1,0:T(8,128)S(1)} %convolution_negate_fusion.1), channel_id=1, source_target_pairs={{0,8},{8,16},{16,24},{24,32},{32,40},{40,48},{48,56},{56,64},{64,7... | collective-permute-start | bytes 1572872 | tf_op jit(solution)/shard_map/ppermute | solution.py:12
  564.7 398.9 %all-gather.14.cloned.1.call-start = ((), (), s32[]{:S(2)}) async-start(), calls=%async_computation.2 | async-start | bytes 1179648 | tf_op jit(solution)/shard_map/all_gather | solution.py:51
  567.0 8.3 collective-permute-start.8
  571.2 9.0 collective-permute-start.9
  827.1 111.4 %copy-start.14 = (f32[128,1024]{1,0:T(8,128)S(1)}, f32[128,1024]{1,0:T(8,128)}, u32[]{:S(2)}) copy-start(f32[128,1024]{1,0:T(8,128)} %copy-done.13) | copy-start | bytes 1572868
  951.6 200.6 %collective-permute-start.5 = (f32[1024,1024]{1,0:T(8,128)}, f32[1024,1024]{1,0:T(8,128)}, u32[]{:S(2)}, u32[]{:S(2)}) collective-permute-start(f32[1024,1024]{1,0:T(8,128)} %all-gather.12.cloned.1.call-done), channel_id=1, source_target_pairs={{16,0},{24,8},{32,16},{40,24},{48,32},{56,40},{64,48},{72,56},{80,... | collective-permute-start | bytes 12582920 | tf_op jit(solution)/shard_map/ppermute | solution.py:12
  963.6 189.8 %copy-start = (f32[1024,1024]{1,0:T(8,128)S(1)}, f32[1024,1024]{1,0:T(8,128)}, u32[]{:S(2)}) copy-start(f32[1024,1024]{1,0:T(8,128)} %get-tuple-element.457) | copy-start | bytes 12582916
  966.0 232.4 %collective-permute-start.10 = (f32[128,256]{1,0:T(8,128)S(1)}, f32[128,256]{1,0:T(8,128)S(1)}, u32[]{:S(2)}, u32[]{:S(2)}) collective-permute-start(f32[128,256]{1,0:T(8,128)S(1)} %fusion.398), channel_id=1, source_target_pairs={{16,0},{24,8},{32,16},{40,24},{48,32},{56,40},{64,48},{72,56},{80,... | collective-permute-start | bytes 393224 | tf_op jit(solution)/shard_map/ppermute | solution.py:12
  975.3 234.5 %collective-permute-start.4 = (f32[128,1024]{0,1:T(8,128)S(1)}, f32[128,1024]{0,1:T(8,128)S(1)}, u32[]{:S(2)}, u32[]{:S(2)}) collective-permute-start(f32[128,1024]{0,1:T(8,128)S(1)} %fusion.396), channel_id=1, source_target_pairs={{16,0},{24,8},{32,16},{40,24},{48,32},{56,40},{64,48},{72,56},{80,... | collective-permute-start | bytes 1572872 | tf_op jit(solution)/shard_map/ppermute | solution.py:12
  1175.1 34.0 %copy-start.16 = (f32[128,256]{1,0:T(8,128)S(1)}, f32[128,256]{1,0:T(8,128)}, u32[]{:S(2)}) copy-start(f32[128,256]{1,0:T(8,128)} %fusion.247) | copy-start | bytes 393220
  1175.2 34.7 %copy-start.4 = (f32[128,1024]{0,1:T(8,128)S(1)}, f32[128,1024]{0,1:T(8,128)}, u32[]{:S(2)}) copy-start(f32[128,1024]{0,1:T(8,128)} %fusion.33) | copy-start | bytes 1572868
  1175.2 34.7 %collective-permute-start.7 = (f32[128,1024]{1,0:T(8,128)S(1)}, f32[128,1024]{1,0:T(8,128)S(1)}, u32[]{:S(2)}, u32[]{:S(2)}) collective-permute-start(f32[128,1024]{1,0:T(8,128)S(1)} %convolution_negate_fusion), channel_id=1, source_target_pairs={{0,16},{8,24},{16,32},{24,40},{32,48},{40,56},{48,64},{56,72},{64,... | collective-permute-start | bytes 1572872 | tf_op jit(solution)/shard_map/ppermute | solution.py:12
  1189.1 20.7 %collective-permute-start.6 = (f32[128,1024]{0,1:T(8,128)S(1)}, f32[128,1024]{0,1:T(8,128)S(1)}, u32[]{:S(2)}, u32[]{:S(2)}) collective-permute-start(f32[128,1024]{0,1:T(8,128)S(1)} %fusion.397), channel_id=1, source_target_pairs={{0,16},{8,24},{16,32},{24,40},{32,48},{40,56},{48,64},{56,72},{64,... | collective-permute-start | bytes 1572872 | tf_op jit(solution)/shard_map/ppermute | solution.py:12
  1194.2 15.0 %collective-permute-start.11 = (f32[128,256]{1,0:T(8,128)S(1)}, f32[128,256]{1,0:T(8,128)S(1)}, u32[]{:S(2)}, u32[]{:S(2)}) collective-permute-start(f32[128,256]{1,0:T(8,128)S(1)} %fusion.399), channel_id=1, source_target_pairs={{0,16},{8,24},{16,32},{24,40},{32,48},{40,56},{48,64},{56,72},{64,... | collective-permute-start | bytes 393224 | tf_op jit(solution)/shard_map/ppermute | solution.py:12
  (16 other events, 101.1 us)
Sparse Core Ops, SparseCore 0:
  10.4 41.4 all-gather.15
  53.8 35.9 all-gather.17
  91.6 25.9 all-gather.19
  543.3 37.1 all-gather.9
  582.8 35.7 all-gather.11
  620.9 26.0 all-gather.13
where the time goes:
time: 1230 us; the launch traced here: 1220 us
  other arithmetic  586 us (48%)
  waiting for transfers between devices  324 us (26%)
  matrix products  156 us (13%)
  local copies, waits for them, and re-layouts  79.8 us (6%)
  starting transfers between devices  45.5 us (4%)
  between operations  27.1 us (2%)
    another operation x59, other arithmetic, split_cholesky(): return jnp.linalg.cholesky(matrix)  332 us
    ppermute x12, waiting for transfers between devices, from_behind(): return lax.ppermute(block, axis, route)  285 us
    another operation x5, other arithmetic, local(): jax.scipy.linalg.cho_solve((factor, True), offdiag_coupling_rows.T)  162 us
    another operation x5, other arithmetic, split_cholesky(): jax.scipy.linalg.solve_triangular(upper_factor, matrix[:half, half:], low...  79.2 us
    another operation x59, local copies, waits for them, and re-layouts, local(): jax.scipy.linalg.cho_solve((factor, True), offdiag_coupling_rows.T)  45.7 us
    another operation x60, matrix products, local(): jax.scipy.linalg.cho_solve((factor, True), offdiag_coupling_rows.T)  45.7 us
    ppermute x12, starting transfers between devices, from_behind(): return lax.ppermute(block, axis, route)  45.2 us
    dot_general x10, matrix products, contract(): lax.dot_general(left, right, (((0,), (0,)), ((), ())), precision=lax.Prec...  39.6 us
  transfers between devices with their start and end apart: 18, of which 7 were waited for; matrix products, arithmetic and copies ran while one was open for 67% of the time, Pallas kernels for 0%

commit v1 on v0

--- a/solution.py
+++ b/solution.py
@@ -2,6 +2,7 @@
 import jax.numpy as jnp
 from jax import lax
 from jax.sharding import PartitionSpec as P
+from jax.lax import all_to_all, axis_size
 
 LEVELS = 2
 
@@ -46,7 +47,15 @@
     for level_step in range(LEVELS):
         level_stride = 1 << level_step
         whole_pivot, whole_coupling, whole_side = (
-            lax.all_gather(diagonal_pivot_rows, "row", axis=0, tiled=True),
+            jnp.concatenate(
+                all_to_all(
+                    jnp.stack([diagonal_pivot_rows for _ in range(axis_size("row"))], axis=0),
+                    "row",
+                    0,
+                    0,
+                ),
+                axis=0,
+            ),
             lax.all_gather(offdiag_coupling_rows, "row", axis=0, tiled=True),
             lax.all_gather(rhs_side_rows, "row", axis=0, tiled=True),
         )

time: 1230 us -> 1320 us (1.073)
  waiting for transfers between devices: 324 us -> 397 us
  local copies, waits for them, and re-layouts: 79.8 us -> 93.3 us
    all_to_all x0 -> x2, waiting for transfers between devices: none -> 102 us  [local(): all_to_all(jnp.stack([diagonal_pivot_rows for _ in range(axis_size('row')...]
    all_gather x2 -> x0, waiting for transfers between devices: 38 us -> none  [local(): lax.all_gather(diagonal_pivot_rows, 'row', axis=0, tiled=True)]
  transfers between devices with their start and end apart: 18 -> 18, of which waited for: 7 -> 8; matrix products, arithmetic and copies ran while one was open for 67% -> 63% of each run, Pallas kernels for 0% -> 0%
where the time goes in v1:
time: 1320 us; the launch traced here: 1310 us
  other arithmetic  578 us (44%)
  waiting for transfers between devices  397 us (30%)
  matrix products  158 us (12%)
  local copies, waits for them, and re-layouts  93.3 us (7%)
  starting transfers between devices  52.1 us (4%)
  between operations  27.4 us (2%)
    another operation x59, other arithmetic, split_cholesky(): return jnp.linalg.cholesky(matrix)  320 us
    ppermute x12, waiting for transfers between devices, from_behind(): return lax.ppermute(block, axis, route)  294 us
    another operation x5, other arithmetic, local(): jax.scipy.linalg.cho_solve((factor, True), offdiag_coupling_rows.T)  164 us
    all_to_all x2, waiting for transfers between devices, local(): all_to_all(jnp.stack([diagonal_pivot_rows for _ in range(axis_size('row')...  102 us
    another operation x5, other arithmetic, split_cholesky(): jax.scipy.linalg.solve_triangular(upper_factor, matrix[:half, half:], low...  80.2 us
    another operation x60, matrix products, local(): jax.scipy.linalg.cho_solve((factor, True), offdiag_coupling_rows.T)  50.8 us
    another operation x59, local copies, waits for them, and re-layouts, local(): jax.scipy.linalg.cho_solve((factor, True), offdiag_coupling_rows.T)  46.6 us
    ppermute x12, starting transfers between devices, from_behind(): return lax.ppermute(block, axis, route)  42.6 us
  transfers between devices with their start and end apart: 18, of which 8 were waited for; matrix products, arithmetic and copies ran while one was open for 63% of the time, Pallas kernels for 0%

profile of v1, /device:TPU:8, one launch (start us, length us, event | category | flops | bytes accessed | tf_op | source)
XLA Modules:
  0.0 1305.3 jit_solution(3608266439759682838)
XLA Ops:
  19.0 64.9 %all-to-all-done = f32[8,128,1024]{1,2,0:T(8,128)} async-done(((f32[8,128,1024]{1,2,0:T(8,128)}), f32[8,128,1024]{1,2,0:T(8,128)}, u32[]{:S(2)}, u32[]{:S(2)}) %all-to-all-start) | async-done | bytes 4194336 | tf_op jit(solution)/shard_map/all_to_all | solution.py:51
  90.5 11.7 cholesky.462
  112.9 11.7 cholesky.481
  135.2 11.7 cholesky.502
  158.1 12.1 cholesky.519
  182.6 39.3 %custom-call.44 = f32[4,128,128]{1,2,0:T(8,128)S(1)} custom-call(f32[4,128,128]{2,1,0:T(8,128)S(1)} %get-tuple-element.46), custom_call_target="InvertDiagBlocksLowerTriangular" | custom-call | tf_op jit(solution)/shard_map/jit(_solve_triangular)/triangular_solve | solution.py:26
  239.2 11.7 cholesky.534
  266.0 13.2 %cholesky.553 = f32[128,128]{1,0:T(8,128)} custom-call(f32[128,128]{1,0:T(8,128)} %cholesky.763), custom_call_target="Cholesky" | custom-call | tf_op jit(solution)/shard_map/jit(cholesky)/cholesky | solution.py:23
  292.8 11.9 cholesky.574
  316.7 11.7 cholesky.591
  334.5 24.2 %while.13 = (s32[]{:T(128)}, f32[1024,1024]{1,0:T(8,128)}, s32[8,2]{0,1:T(2,128)S(1)}, f32[8,128,128]{2,1,0:T(8,128)S(1)}, s32[]{:T(128)}) while((s32[]{:T(128)}, f32[1024,1024]{1,0:T(8,128)}, s32[8,2]{0,1:T(2,128)S(1)}, f32[8,128,128]{2,1,0:T(8,128)S(1)}, s32[]{:T(128)}) %tuple.192), condition=%wide.while_cond.1, body=%wide.while_body.1.sunk | while | flops 2 | bytes 131181 | solution.py:64
  358.6 78.8 %custom-call.48 = f32[8,128,128]{1,2,0:T(8,128)S(1)} custom-call(f32[8,128,128]{2,1,0:T(8,128)S(1)} %get-tuple-element.47), custom_call_target="InvertDiagBlocksLowerTriangular" | custom-call | tf_op jit(solution)/shard_map/jit(_cho_solve)/triangular_solve | solution.py:64
  481.6 75.7 %collective-permute-done.1 = f32[1024,1024]{1,0:T(8,128)S(1)} collective-permute-done((f32[1024,1024]{1,0:T(8,128)}, f32[1024,1024]{1,0:T(8,128)S(1)}, u32[]{:S(2)}, u32[]{:S(2)}) %collective-permute-start.1) | collective-permute-done | bytes 4194336 | tf_op jit(solution)/shard_map/ppermute | solution.py:13
  570.9 11.8 collective-permute-done.3
  592.4 12.6 collective-permute-done.2
  630.2 36.9 %all-to-all-done.1 = f32[8,128,1024]{1,2,0:T(8,128)} async-done(((f32[8,128,1024]{1,2,0:T(8,128)}), f32[8,128,1024]{1,2,0:T(8,128)}, u32[]{:S(2)}, u32[]{:S(2)}) %all-to-all-start.1) | async-done | bytes 4194336 | tf_op jit(solution)/shard_map/all_to_all | solution.py:51
  742.8 12.1 cholesky.663
  759.7 12.0 while.14
  771.7 39.3 %custom-call.53 = f32[4,128,128]{1,2,0:T(8,128)S(1)} custom-call(f32[4,128,128]{2,1,0:T(8,128)S(1)} %get-tuple-element.49), custom_call_target="InvertDiagBlocksLowerTriangular" | custom-call | tf_op jit(solution)/shard_map/jit(_solve_triangular)/triangular_solve | solution.py:26
  878.3 12.1 cholesky.718
  921.3 22.6 %while.15 = (s32[]{:T(128)}, f32[1024,1024]{1,0:T(8,128)}, s32[8,2]{0,1:T(2,128)S(1)}, f32[8,128,128]{2,1,0:T(8,128)S(1)}, s32[]{:T(128)}) while((s32[]{:T(128)}, f32[1024,1024]{1,0:T(8,128)}, s32[8,2]{0,1:T(2,128)S(1)}, f32[8,128,128]{2,1,0:T(8,128)S(1)}, s32[]{:T(128)}) %tuple.211), condition=%wide.while_cond.1.clone.1, body=%wide.while_body.1.clone.1.sunk | while | flops 2 | bytes 131181 | solution.py:64
  943.9 78.8 %custom-call.57 = f32[8,128,128]{1,2,0:T(8,128)S(1)} custom-call(f32[8,128,128]{2,1,0:T(8,128)S(1)} %get-tuple-element.50), custom_call_target="InvertDiagBlocksLowerTriangular" | custom-call | tf_op jit(solution)/shard_map/jit(_cho_solve)/triangular_solve | solution.py:64
  1065.7 174.7 %collective-permute-done.5 = f32[1024,1024]{1,0:T(8,128)} collective-permute-done((f32[1024,1024]{1,0:T(8,128)}, f32[1024,1024]{1,0:T(8,128)}, u32[]{:S(2)}, u32[]{:S(2)}) %collective-permute-start.5) | collective-permute-done | bytes 4194336 | tf_op jit(solution)/shard_map/ppermute | solution.py:13
  1282.0 13.9 %collective-permute-done.11 = f32[128,256]{1,0:T(8,128)S(1)} collective-permute-done((f32[128,256]{1,0:T(8,128)S(1)}, f32[128,256]{1,0:T(8,128)S(1)}, u32[]{:S(2)}, u32[]{:S(2)}) %collective-permute-start.11) | collective-permute-done | bytes 131104 | tf_op jit(solution)/shard_map/ppermute | solution.py:13
  (518 shorter events, 539.0 us)
Async XLA Ops:
  7.2 450.9 %all-gather.11.cloned.1.call-start = ((), (), s32[]{:S(2)}) async-start(), calls=%async_computation.4 | async-start | bytes 4718592 | tf_op jit(solution)/shard_map/all_gather | solution.py:59
  12.6 71.2 %all-to-all-start = ((f32[8,128,1024]{1,2,0:T(8,128)}), f32[8,128,1024]{1,2,0:T(8,128)}, u32[]{:S(2)}, u32[]{:S(2)}) async-start(f32[8,128,1024]{1,2,0:T(8,128)} %stack.4), calls=%async_computation | async-start | bytes 8388608 | tf_op jit(solution)/shard_map/all_to_all | solution.py:51
  17.3 596.1 %all-gather.13.cloned.1.call-start = ((), (), s32[]{:S(2)}) async-start(), calls=%async_computation.5 | async-start | bytes 1179648 | tf_op jit(solution)/shard_map/all_gather | solution.py:60
  18.1 1024.3 %all-gather.7.cloned.1.call-start = ((), (), s32[]{:S(2)}) async-start(), calls=%async_computation.2 | async-start | bytes 4718592 | tf_op jit(solution)/shard_map/all_gather | solution.py:59
  458.1 99.3 %collective-permute-start.1 = (f32[1024,1024]{1,0:T(8,128)}, f32[1024,1024]{1,0:T(8,128)S(1)}, u32[]{:S(2)}, u32[]{:S(2)}) collective-permute-start(f32[1024,1024]{1,0:T(8,128)} %bitcast.480), channel_id=1, source_target_pairs={{8,0},{16,8},{24,16},{32,24},{40,32},{48,40},{56,48},{64,56},{72,6... | collective-permute-start | bytes 12582920 | tf_op jit(solution)/shard_map/ppermute | solution.py:13
  478.5 113.9 %collective-permute-start = (f32[128,1024]{1,0:T(8,128)S(1)}, f32[128,1024]{1,0:T(8,128)}, u32[]{:S(2)}, u32[]{:S(2)}) collective-permute-start(f32[128,1024]{1,0:T(8,128)S(1)} %fusion.384), channel_id=1, source_target_pairs={{8,0},{16,8},{24,16},{32,24},{40,32},{48,40},{56,48},{64,56},{72,6... | collective-permute-start | bytes 1572872 | tf_op jit(solution)/shard_map/ppermute | solution.py:13
  566.9 15.8 %collective-permute-start.3 = (f32[128,1024]{1,0:T(8,128)S(1)}, f32[128,1024]{1,0:T(8,128)S(1)}, u32[]{:S(2)}, u32[]{:S(2)}) collective-permute-start(f32[128,1024]{1,0:T(8,128)S(1)} %convolution_negate_fusion.1), channel_id=1, source_target_pairs={{0,8},{8,16},{16,24},{24,32},{32,40},{40,48},{48,56},{56,64},{64,7... | collective-permute-start | bytes 1572872 | tf_op jit(solution)/shard_map/ppermute | solution.py:13
  585.5 19.5 %copy-start.14 = (f32[1,128,1024]{2,1,0:T(8,128)S(1)}, f32[1,128,1024]{2,1,0:T(8,128)}, u32[]{:S(2)}) copy-start(f32[1,128,1024]{2,1,0:T(8,128)} %param.8) | copy-start | bytes 1572868
  590.5 14.5 %collective-permute-start.2 = (f32[128,1024]{1,0:T(8,128)S(1)}, f32[128,1024]{1,0:T(8,128)S(1)}, u32[]{:S(2)}, u32[]{:S(2)}) collective-permute-start(f32[128,1024]{1,0:T(8,128)S(1)} %fusion.390), channel_id=1, source_target_pairs={{0,8},{8,16},{16,24},{24,32},{32,40},{40,48},{48,56},{56,64},{64,7... | collective-permute-start | bytes 1572872 | tf_op jit(solution)/shard_map/ppermute | solution.py:13
  608.6 20.9 %copy-start.16 = (f32[1,128,256]{2,1,0:T(8,128)S(1)}, f32[1,128,256]{2,1,0:T(8,128)}, u32[]{:S(2)}) copy-start(f32[1,128,256]{2,1,0:T(8,128)} %param.10) | copy-start | bytes 393220
  608.6 58.6 %all-to-all-start.1 = ((f32[8,128,1024]{1,2,0:T(8,128)}), f32[8,128,1024]{1,2,0:T(8,128)}, u32[]{:S(2)}, u32[]{:S(2)}) async-start(f32[8,128,1024]{1,2,0:T(8,128)} %stack.5), calls=%async_computation.1 | async-start | bytes 8388608 | tf_op jit(solution)/shard_map/all_to_all | solution.py:51
  613.3 437.3 %all-gather.9.cloned.1.call-start = ((), (), s32[]{:S(2)}) async-start(), calls=%async_computation.3 | async-start | bytes 1179648 | tf_op jit(solution)/shard_map/all_gather | solution.py:60
  615.7 8.5 collective-permute-start.8
  619.9 9.7 collective-permute-start.9
  917.5 105.2 %copy-start.12 = (f32[128,1024]{1,0:T(8,128)S(1)}, f32[128,1024]{1,0:T(8,128)}, u32[]{:S(2)}) copy-start(f32[128,1024]{1,0:T(8,128)} %copy-done.11) | copy-start | bytes 1572868
  1042.3 198.1 %collective-permute-start.5 = (f32[1024,1024]{1,0:T(8,128)}, f32[1024,1024]{1,0:T(8,128)}, u32[]{:S(2)}, u32[]{:S(2)}) collective-permute-start(f32[1024,1024]{1,0:T(8,128)} %all-gather.7.cloned.1.call-done), channel_id=1, source_target_pairs={{16,0},{24,8},{32,16},{40,24},{48,32},{56,40},{64,48},{72,56},{80,... | collective-permute-start | bytes 12582920 | tf_op jit(solution)/shard_map/ppermute | solution.py:13
  1050.6 190.9 %copy-start = (f32[1024,1024]{1,0:T(8,128)S(1)}, f32[1024,1024]{1,0:T(8,128)}, u32[]{:S(2)}) copy-start(f32[1024,1024]{1,0:T(8,128)} %get-tuple-element.452) | copy-start | bytes 12582916
  1053.0 229.0 %collective-permute-start.10 = (f32[128,256]{1,0:T(8,128)S(1)}, f32[128,256]{1,0:T(8,128)S(1)}, u32[]{:S(2)}, u32[]{:S(2)}) collective-permute-start(f32[128,256]{1,0:T(8,128)S(1)} %fusion.393), channel_id=1, source_target_pairs={{16,0},{24,8},{32,16},{40,24},{48,32},{56,40},{64,48},{72,56},{80,... | collective-permute-start | bytes 393224 | tf_op jit(solution)/shard_map/ppermute | solution.py:13
  1063.2 233.3 %collective-permute-start.4 = (f32[128,1024]{1,0:T(8,128)S(1)}, f32[128,1024]{1,0:T(8,128)S(1)}, u32[]{:S(2)}, u32[]{:S(2)}) collective-permute-start(f32[128,1024]{1,0:T(8,128)S(1)} %fusion.391), channel_id=1, source_target_pairs={{16,0},{24,8},{32,16},{40,24},{48,32},{56,40},{64,48},{72,56},{80,... | collective-permute-start | bytes 1572872 | tf_op jit(solution)/shard_map/ppermute | solution.py:13
  1258.6 16.8 %copy-start.6 = (f32[1024,256]{1,0:T(8,128)S(1)}, f32[1024,256]{1,0:T(8,128)}, u32[]{:S(2)}) copy-start(f32[1024,256]{1,0:T(8,128)} %all-gather.9.cloned.1.call-done) | copy-start | bytes 3145732
  1263.3 32.6 %copy-start.15 = (f32[128,256]{1,0:T(8,128)S(1)}, f32[128,256]{1,0:T(8,128)}, u32[]{:S(2)}) copy-start(f32[128,256]{1,0:T(8,128)} %fusion.240) | copy-start | bytes 393220
  1263.3 33.3 %collective-permute-start.7 = (f32[128,1024]{1,0:T(8,128)S(1)}, f32[128,1024]{1,0:T(8,128)S(1)}, u32[]{:S(2)}, u32[]{:S(2)}) collective-permute-start(f32[128,1024]{1,0:T(8,128)S(1)} %convolution_negate_fusion), channel_id=1, source_target_pairs={{0,16},{8,24},{16,32},{24,40},{32,48},{40,56},{48,64},{56,72},{64,... | collective-permute-start | bytes 1572872 | tf_op jit(solution)/shard_map/ppermute | solution.py:13
  1271.8 24.8 %collective-permute-start.6 = (f32[128,1024]{1,0:T(8,128)S(1)}, f32[128,1024]{1,0:T(8,128)S(1)}, u32[]{:S(2)}, u32[]{:S(2)}) collective-permute-start(f32[128,1024]{1,0:T(8,128)S(1)} %fusion.392), channel_id=1, source_target_pairs={{0,16},{8,24},{16,32},{24,40},{32,48},{40,56},{48,64},{56,72},{64,... | collective-permute-start | bytes 1572872 | tf_op jit(solution)/shard_map/ppermute | solution.py:13
  1276.5 19.4 %collective-permute-start.11 = (f32[128,256]{1,0:T(8,128)S(1)}, f32[128,256]{1,0:T(8,128)S(1)}, u32[]{:S(2)}, u32[]{:S(2)}) collective-permute-start(f32[128,256]{1,0:T(8,128)S(1)} %fusion.394), channel_id=1, source_target_pairs={{0,16},{8,24},{16,32},{24,40},{32,48},{40,56},{48,64},{56,72},{64,... | collective-permute-start | bytes 393224 | tf_op jit(solution)/shard_map/ppermute | solution.py:13
  (14 other events, 51.6 us)
Sparse Core Ops, SparseCore 0:
  10.4 59.2 all-gather.10
  71.6 25.5 all-gather.12
  583.7 31.5 all-gather.6
  630.4 25.9 all-gather.8
